TPU v7x, 256 devices: a whole 4x4x8 slice. The times are simulated.
256 devices in a mesh: row: 16 (over y, x), col: 16 (over z, core).
Axes of the slice: x: 4, y: 4, z: 8, core: 2. Of those that a mesh axis runs over, the one named last changes fastest.
Arguments:
- features: bfloat16 [512, 512, 128], P('col')
- diag_inverse: bfloat16 [512, 128, 128], P('col')
- precision_tiles: float32 [16, 16, 32, 128, 128], P('row', 'col'), may hold values from -3 to 3
- inverse_tiles: float32 [16, 16, 32, 128, 128], P('row', 'col'), may hold values from -0.3125 to 0.3125
- slot_rows: int32 [16, 16, 32], replicated, may hold values from 0 to 511, as said below
- slot_columns: int32 [16, 16, 32], replicated, may hold values from 0 to 1, as said below
- owned_columns: int32 [16, 16, 2], replicated, may hold values from 0 to 511, as said below
- live_counts: int32 [16, 16], replicated, may hold values from 1 to 32, as said below
Outputs:
- direction: float32 [16, 16, 32, 128, 128], P('row', 'col')
Inputs may be any that keep to these rules, and one draw needn't show every extreme that they name: `slot_rows`: slot k of every owner names a block-row held by index k // 2 of col, that is one of feature blocks 32 * (k // 2) to 32 * (k // 2) + 31; no pair of block-row and block-column is named by two slots of the whole grid. `slot_columns`: some owner uses every entry of its list. `owned_columns`: an owner's 2 block-columns are distinct and lie among the feature blocks of its own index of col. The live slots of an owner are slots 0 to live_counts - 1; some owner has all 32 slots live.
All inputs are finite; a program needn't handle non-finite values.
Results may differ from a plain program's by a relative error of at most 0.0003.
Values may be sent and summed in bfloat16 or wider, within the bound.
No kernel may reach another device: no remote copies, remote signals or barrier semaphores. Data moves between devices by JAX's collectives and lax.ppermute only.
A program may use at most 128 MiB of HBM per device.

v0:
```python
import jax
import jax.numpy as jnp
from jax import lax
from jax.sharding import PartitionSpec as P

SWEEPS = 4
step_size = 0.3
penalty = 0.6
highest = lax.Precision.HIGHEST


def soft_update(precision_tile, direction, residual):
    shifted = precision_tile + direction - step_size * residual
    return (
        jnp.sign(shifted) * jnp.maximum(jnp.abs(shifted) - step_size * penalty, 0.0)
        - precision_tile
    )


def body(
    features,
    diag_inverse,
    precision_tiles,
    inverse_tiles,
    slot_rows,
    slot_columns,
    owned_columns,
    live_counts,
):
    col_count = lax.axis_size("col")
    row_index = lax.axis_index("row")
    col_index = lax.axis_index("col")
    block_count = features.shape[0]
    sample_count = features.shape[1]
    block_size = features.shape[2]
    slot_count = precision_tiles.shape[2]
    per_source = slot_count // col_count
    row_table = slot_rows[row_index]
    wanted = jnp.take(row_table.reshape(col_count, col_count, per_source), col_index, axis=1)
    local_rows = (wanted - col_index * block_count).reshape(-1)
    send_tiles = jnp.take(features, local_rows, axis=0).reshape(
        col_count, per_source, sample_count, block_size
    )
    send_diag = jnp.take(diag_inverse, local_rows, axis=0).reshape(
        col_count, per_source, block_size, block_size
    )
    row_tiles, row_diag = (
        lax.all_to_all(send_tiles, "col", split_axis=0, concat_axis=0, tiled=True),
        lax.all_to_all(send_diag, "col", split_axis=0, concat_axis=0, tiled=True),
    )
    row_tiles = row_tiles.reshape(slot_count, sample_count, block_size)
    row_diag = row_diag.reshape(slot_count, block_size, block_size).astype(jnp.float32)
    my_lists = slot_columns[row_index, col_index]
    my_owned = owned_columns[row_index, col_index]
    column_ids = jnp.take(my_owned, my_lists)
    local_cols = column_ids - col_index * block_count
    live_mask = (jnp.arange(slot_count) < live_counts[row_index, col_index]).astype(jnp.float32)
    col_tiles = jnp.take(features, local_cols, axis=0)
    covariance = (
        jnp.einsum("kna,knb->kab", row_tiles, col_tiles, preferred_element_type=jnp.float32)
        / sample_count
    )
    tiles_here = inverse_tiles[0, 0]
    theta_here = precision_tiles[0, 0]
    gradient = covariance - tiles_here
    col_diag = jnp.take(diag_inverse, local_cols, axis=0).astype(jnp.float32)
    direction = jnp.zeros_like(gradient)
    for sweep_index in range(SWEEPS):
        residual = gradient
        if sweep_index > 0:
            left_side = jnp.einsum("kab,kbc->kac", row_diag, direction, precision=highest)
            residual = residual + jnp.einsum("kac,kcd->kad", left_side, col_diag, precision=highest)
            products = (
                jnp.einsum("kba,kbc->kac", direction, tiles_here, precision=highest)
                * live_mask[:, None, None]
            )
            onehot = (local_cols[:, None] == jnp.arange(block_count)[None, :]).astype(jnp.float32)
            dense_sums = jnp.einsum("kf,kab->fab", onehot, products, precision=highest)
            summed = lax.psum(dense_sums, "row")
            residual = residual + jnp.einsum(
                "kab,kbc->kac",
                tiles_here,
                jnp.einsum("kf,fab->kab", onehot, summed, precision=highest),
                precision=highest,
            )
        direction = soft_update(theta_here, direction, residual)
    return (direction * live_mask[:, None, None]).reshape(precision_tiles.shape)


def solution(mesh):
    return jax.shard_map(
        body,
        mesh=mesh,
        in_specs=(
            P("col", None, None),
            P("col", None, None),
            P("row", "col", None, None, None),
            P("row", "col", None, None, None),
            P(),
            P(),
            P(),
            P(),
        ),
        out_specs=P("row", "col", None, None, None),
        check_vma=False,
    )
```

profile of v0, /device:TPU:1, one launch (start us, length us, event | category | flops | bytes accessed | tf_op | source)
XLA Modules:
  0.0 511.0 jit_solution(2454693895170861494)
XLA Ops:
  10.9 5.2 %gather_fusion = bf16[32,512,128]{2,1,0:T(8,128)(2,1)} fusion(bf16[32,512,128]{2,1,0:T(8,128)(2,1)} %param.12, s32[1024]{0:T(1024)S(1)} %pad_clamp_fusion.1), kind=kCustom, calls=%fused_computation.clone | custom fusion | bytes 8388736 | tf_op jit(solution)/shard_map/jit(_take)/gather | solution.py:41
  16.1 4.6 broadcast_select_fusion
  20.7 6.5 %copy.15 = bf16[16,2,512,128]{2,3,1,0:T(8,128)(2,1)} copy(bf16[16,2,512,128]{3,2,1,0:T(8,128)(2,1)} %bitcast.129) | data formatting | bytes 8388608 | tf_op jit(solution)/shard_map/reshape | solution.py:41
  27.2 10.0 %all-to-all-start = ((bf16[16,2,512,128]{2,3,1,0:T(8,128)(2,1)}), bf16[16,2,512,128]{2,3,1,0:T(8,128)(2,1)}, u32[]{:S(2)}, u32[]{:S(2)}) async-start(bf16[16,2,512,128]{2,3,1,0:T(8,128)(2,1)} %copy.15), calls=%async_computation | async-start | bytes 8388608 | tf_op jit(solution)/shard_map/all_to_all | solution.py:48
  40.1 5.2 %gather_fusion.1 = bf16[32,512,128]{2,1,0:T(8,128)(2,1)} fusion(bf16[32,512,128]{2,1,0:T(8,128)(2,1)} %param.12, s32[1024]{0:T(1024)S(1)} %pad_clamp_fusion), kind=kCustom, calls=%fused_computation.2.clone | custom fusion | bytes 8388736 | tf_op jit(solution)/shard_map/jit(_take)/gather | solution.py:58
  45.9 2.5 broadcast_select_fusion.2
  48.5 82.3 %all-to-all-done = bf16[16,2,512,128]{2,3,1,0:T(8,128)(2,1)} async-done(((bf16[16,2,512,128]{2,3,1,0:T(8,128)(2,1)}), bf16[16,2,512,128]{2,3,1,0:T(8,128)(2,1)}, u32[]{:S(2)}, u32[]{:S(2)}) %all-to-all-start) | async-done | bytes 4194336 | tf_op jit(solution)/shard_map/all_to_all | solution.py:48
  130.7 5.5 %all-to-all-start.1 = ((bf16[16,2,128,128]{3,2,1,0:T(8,128)(2,1)}), bf16[16,2,128,128]{3,2,1,0:T(8,128)(2,1)}, u32[]{:S(2)}, u32[]{:S(2)}) async-start(bf16[16,2,128,128]{3,2,1,0:T(8,128)(2,1)} %bitcast.130), calls=%async_computation.1 | async-start | bytes 2097152 | tf_op jit(solution)/shard_map/all_to_all | solution.py:49
  136.5 4.9 bitcast_subtract_fusion
  141.5 4.5 fusion.39
  148.5 2.5 copy.20
  153.0 11.3 %all-to-all-done.1 = bf16[16,2,128,128]{3,2,1,0:T(8,128)(2,1)} async-done(((bf16[16,2,128,128]{3,2,1,0:T(8,128)(2,1)}), bf16[16,2,128,128]{3,2,1,0:T(8,128)(2,1)}, u32[]{:S(2)}, u32[]{:S(2)}) %all-to-all-start.1) | async-done | bytes 1048608 | tf_op jit(solution)/shard_map/all_to_all | solution.py:49
  164.3 4.8 fusion.62
  169.1 2.6 fusion.87
  171.7 79.8 %all-reduce.4.cloned.1.call-done = f32[32,128,128]{2,1,0:T(8,128)} async-done(((f32[32,128,128]{2,1,0:T(8,128)}), f32[32,128,128]{2,1,0:T(8,128)}) %all-reduce.4.cloned.1.call-update) | async-done | bytes 2097168 | tf_op jit(solution)/shard_map/psum | solution.py:79
  251.5 4.1 fusion.34
  255.6 6.9 %bitcast_subtract_fusion.3 = f32[32,128,128]{2,1,0:T(8,128)S(1)} fusion(f32[1,1,32,128,128]{4,3,2,1,0:T(8,128)S(1)} %copy-done.4, f32[32,128,128]{2,1,0:T(8,128)S(1)} %copy-done.8, f32[32,128,128]{2,1,0:T(8,128)} %fusion.87, f32[1,1,32,128,128]{4,3,2,1,0:T(8,128)S(1)} %copy-done.2, f32[32,128,128]{2,0,1:T(8,128)S(1)} %fusion.34), kind=kOutput, calls=%fused_computation.34 | convolution fusion | flops 815267840 | bytes 12582912 | tf_op jit(solution)/shard_map/kab,kbc->kac/dot_general | solution.py:80
  262.5 4.3 fusion.42
  266.8 2.5 fusion.31
  269.3 2.6 copy.25
  272.0 3.2 fusion.90
  275.1 2.5 fusion.86
  277.7 94.3 %all-reduce.6.cloned.1.call-done = f32[32,128,128]{2,1,0:T(8,128)} async-done(((f32[32,128,128]{2,1,0:T(8,128)}), f32[32,128,128]{2,1,0:T(8,128)}) %all-reduce.6.cloned.1.call-update) | async-done | bytes 2097168 | tf_op jit(solution)/shard_map/psum | solution.py:79
  371.9 4.1 fusion.29
  376.0 6.9 %bitcast_subtract_fusion.2 = f32[32,128,128]{2,1,0:T(8,128)S(1)} fusion(f32[1,1,32,128,128]{4,3,2,1,0:T(8,128)S(1)} %copy-done.5, f32[32,128,128]{2,1,0:T(8,128)} %copy-done.12, f32[32,128,128]{2,1,0:T(8,128)S(1)} %copy-done.9, f32[32,128,128]{2,1,0:T(8,128)} %fusion.86, f32[1,1,32,128,128]{4,3,2,1,0:T(8,128)S(1)} %copy-done.2, f32[32,128,128]{2,0,1:T(8,128)S(1)} %fusion.29), kind=kOutput, calls=%fused_computation.32 | convolution fusion | flops 811073536 | bytes 14680064 | tf_op jit(solution)/shard_map/kab,kbc->kac/dot_general | solution.py:80
  383.0 4.0 fusion.45
  389.5 2.6 copy.30
  392.1 3.2 fusion.91
  395.3 2.6 fusion.85
  397.8 94.2 %all-reduce.8.cloned.1.call-done = f32[32,128,128]{2,1,0:T(8,128)} async-done(((f32[32,128,128]{2,1,0:T(8,128)}), f32[32,128,128]{2,1,0:T(8,128)}) %all-reduce.8.cloned.1.call-update) | async-done | bytes 2097168 | tf_op jit(solution)/shard_map/psum | solution.py:79
  492.0 4.3 fusion.24
  496.4 7.9 %fusion.22 = f32[1,1,32,128,128]{4,3,2,1,0:T(8,128)} fusion(f32[1,1,32,128,128]{4,3,2,1,0:T(8,128)S(1)} %copy-done.6, f32[32,128,128]{2,1,0:T(8,128)} %copy-done.11, f32[32,128,128]{2,1,0:T(8,128)S(1)} %copy-done.10, f32[32,128,128]{2,1,0:T(8,128)} %fusion.85, f32[1,1,32,128,128]{4,3,2,1,0:T(8,128)S(1)} %copy-done.2, f32[32,128,128]{2,0,1:T(8,128)S(1)} %fusion.24, ...), kind=kOutput, calls=%fused_computation.39 | convolution fusion | flops 811597824 | bytes 14680192 | tf_op jit(solution)/shard_map/kab,kbc->kac/dot_general | solution.py:80
  (52 shorter events, 15.2 us)
Async XLA Ops:
  6.5 31.9 %copy-start = (bf16[32,128,128]{2,1,0:T(8,128)(2,1)S(1)}, bf16[32,128,128]{2,1,0:T(8,128)(2,1)}, u32[]{:S(2)}) copy-start(bf16[32,128,128]{2,1,0:T(8,128)(2,1)} %param.13) | copy-start | bytes 3145732
  27.2 103.6 %all-to-all-start = ((bf16[16,2,512,128]{2,3,1,0:T(8,128)(2,1)}), bf16[16,2,512,128]{2,3,1,0:T(8,128)(2,1)}, u32[]{:S(2)}, u32[]{:S(2)}) async-start(bf16[16,2,512,128]{2,3,1,0:T(8,128)(2,1)} %copy.15), calls=%async_computation | async-start | bytes 8388608 | tf_op jit(solution)/shard_map/all_to_all | solution.py:48
  45.9 90.6 %copy-start.2 = (f32[1,1,32,128,128]{4,3,2,1,0:T(8,128)S(1)}, f32[1,1,32,128,128]{4,3,2,1,0:T(8,128)}, u32[]{:S(2)}) copy-start(f32[1,1,32,128,128]{4,3,2,1,0:T(8,128)} %param.15) | copy-start | bytes 6291460
  130.7 33.6 %all-to-all-start.1 = ((bf16[16,2,128,128]{3,2,1,0:T(8,128)(2,1)}), bf16[16,2,128,128]{3,2,1,0:T(8,128)(2,1)}, u32[]{:S(2)}, u32[]{:S(2)}) async-start(bf16[16,2,128,128]{3,2,1,0:T(8,128)(2,1)} %bitcast.130), calls=%async_computation.1 | async-start | bytes 2097152 | tf_op jit(solution)/shard_map/all_to_all | solution.py:49
  136.3 115.2 %all-reduce.4.cloned.1.call-start = ((), (), s32[]{:S(2)}) async-start(), calls=%async_computation.2 | async-start | bytes 4194304 | tf_op jit(solution)/shard_map/psum | solution.py:79
  136.5 4.9 copy-start.3
  141.4 4.5 copy-start.7
  151.0 220.9 %all-reduce.6.cloned.1.call-start = ((), (), s32[]{:S(2)}) async-start(), calls=%async_computation.3 | async-start | bytes 4194304 | tf_op jit(solution)/shard_map/psum | solution.py:79
  164.3 4.8 copy-start.13
  251.5 4.1 copy-start.4
  251.5 4.1 copy-start.8
  262.5 4.3 copy-start.12
  271.9 220.1 %all-reduce.8.cloned.1.call-start = ((), (), s32[]{:S(2)}) async-start(), calls=%async_computation.4 | async-start | bytes 4194304 | tf_op jit(solution)/shard_map/psum | solution.py:79
  371.9 4.1 copy-start.5
  371.9 4.1 copy-start.9
  383.0 4.0 copy-start.11
  492.0 4.3 copy-start.6
  492.0 4.3 copy-start.10
  496.4 7.9 %copy-start.1 = (bf16[32,128,128]{2,1,0:T(8,128)(2,1)S(1)}, bf16[32,128,128]{2,1,0:T(8,128)(2,1)}, u32[]{:S(2)}) copy-start(bf16[32,128,128]{2,1,0:T(8,128)(2,1)} %param.13) | copy-start | bytes 3145732
Sparse Core Ops, SparseCore 0:
  151.2 100.2 all-reduce.3
  272.0 99.8 all-reduce.5
  392.2 99.7 all-reduce.7
where the time goes:
time: 514 us; the launch traced here: 511 us
  waiting for transfers between devices  362 us (70%)
  matrix products  78.1 us (15%)
  local copies, waits for them, and re-layouts  31.6 us (6%)
  starting transfers between devices  16 us (3%)
  between operations  13.6 us (3%)
  other arithmetic  9.75 us (2%)
    psum x3, waiting for transfers between devices, body(): summed = lax.psum(dense_sums, 'row')  268 us
    all_to_all x1, waiting for transfers between devices, body(): lax.all_to_all(send_tiles, 'col', split_axis=0, concat_axis=0, tiled=True)  82.3 us
    dot_general x3, matrix products, body(): jnp.einsum('kab,kbc->kac', tiles_here, jnp.einsum('kf,fab->kab', onehot,...  21.7 us
    dot_general x3, matrix products, body(): jnp.einsum('kba,kbc->kac', direction, tiles_here, precision=highest)  12.8 us
    dot_general x3, matrix products, body(): jnp.einsum('kf,fab->kab', onehot, summed, precision=highest)  12.4 us
    all_to_all x1, waiting for transfers between devices, body(): lax.all_to_all(send_diag, 'col', split_axis=0, concat_axis=0, tiled=True)  11.3 us
    dot_general x3, matrix products, body(): jnp.einsum('kab,kbc->kac', row_diag, direction, precision=highest)  11.1 us
  transfers between devices with their start and end apart: 5, of which 5 were waited for; matrix products, arithmetic and copies ran while one was open for 9% of the time, Pallas kernels for 0%

commit v1 on v0

--- a/solution.py
+++ b/solution.py
@@ -76,7 +76,11 @@
             )
             onehot = (local_cols[:, None] == jnp.arange(block_count)[None, :]).astype(jnp.float32)
             dense_sums = jnp.einsum("kf,kab->fab", onehot, products, precision=highest)
-            summed = lax.psum(dense_sums, "row")
+            summed = dense_sums
+            for hop in (1, 2, 4, 8):
+                summed = summed + lax.ppermute(
+                    summed, "row", [(dev, dev ^ hop) for dev in range(16)]
+                )
             residual = residual + jnp.einsum(
                 "kab,kbc->kac",
                 tiles_here,

time: 514 us -> 736 us (1.43)
  the two profiles are of different devices: /device:TPU:1 before, /device:TPU:62 now
where the time goes in v1:
time: 736 us; the launch traced here: 727 us
  waiting for transfers between devices  576 us (78%)
  matrix products  60.5 us (8%)
  starting transfers between devices  47.4 us (6%)
  local copies, waits for them, and re-layouts  24 us (3%)
  other arithmetic  18.7 us (3%)
    ppermute x12, waiting for transfers between devices, body(): lax.ppermute(summed, 'row', [(dev, dev ^ hop) for dev in range(16)])  491 us
    all_to_all x1, waiting for transfers between devices, body(): lax.all_to_all(send_tiles, 'col', split_axis=0, concat_axis=0, tiled=True)  85.1 us
    ppermute x12, starting transfers between devices, body(): lax.ppermute(summed, 'row', [(dev, dev ^ hop) for dev in range(16)])  32.7 us
    dot_general x3, matrix products, body(): jnp.einsum('kab,kbc->kac', tiles_here, jnp.einsum('kf,fab->kab', onehot,...  15.8 us
  transfers between devices with their start and end apart: 14, of which 13 were waited for; matrix products, arithmetic and copies ran while one was open for 4% of the time, Pallas kernels for 0%

profile of v1, /device:TPU:62, one launch (start us, length us, event | category | flops | bytes accessed | tf_op | source)
XLA Modules:
  0.0 727.0 jit_solution(5110879044679770878)
XLA Ops:
  4.3 5.3 gather_fusion
  9.6 4.7 broadcast_select_fusion
  14.3 6.4 copy.18
  20.6 8.6 %all-to-all-start = ((bf16[16,2,512,128]{2,3,1,0:T(8,128)(2,1)}), bf16[16,2,512,128]{2,3,1,0:T(8,128)(2,1)}, u32[]{:S(2)}, u32[]{:S(2)}) async-start(bf16[16,2,512,128]{2,3,1,0:T(8,128)(2,1)} %copy.18), calls=%async_computation | async-start | bytes 8388608 | tf_op jit(solution)/shard_map/all_to_all | solution.py:48
  29.3 5.4 gather_fusion.1
  36.6 85.1 %all-to-all-done = bf16[16,2,512,128]{2,3,1,0:T(8,128)(2,1)} async-done(((bf16[16,2,512,128]{2,3,1,0:T(8,128)(2,1)}), bf16[16,2,512,128]{2,3,1,0:T(8,128)(2,1)}, u32[]{:S(2)}, u32[]{:S(2)}) %all-to-all-start) | async-done | bytes 4194336 | tf_op jit(solution)/shard_map/all_to_all | solution.py:48
  121.7 4.9 bitcast_subtract_fusion
  126.7 4.5 fusion.39
  134.6 47.0 %collective-permute-done = f32[32,128,128]{2,0,1:T(8,128)S(1)} collective-permute-done((f32[32,128,128]{2,0,1:T(8,128)S(1)}, f32[32,128,128]{2,0,1:T(8,128)S(1)}, u32[]{:S(2)}, u32[]{:S(2)}) %collective-permute-start) | collective-permute-done | bytes 2097184 | tf_op jit(solution)/shard_map/ppermute | solution.py:81
  183.8 47.1 %collective-permute-done.1 = f32[32,128,128]{2,0,1:T(8,128)S(1)} collective-permute-done((f32[32,128,128]{2,0,1:T(8,128)S(1)}, f32[32,128,128]{2,0,1:T(8,128)S(1)}, u32[]{:S(2)}, u32[]{:S(2)}) %collective-permute-start.1) | collective-permute-done | bytes 2097184 | tf_op jit(solution)/shard_map/ppermute | solution.py:81
  237.4 6.1 all-to-all-start.1
  243.5 35.6 %collective-permute-done.2 = f32[32,128,128]{2,0,1:T(8,128)} collective-permute-done((f32[32,128,128]{2,0,1:T(8,128)}, f32[32,128,128]{2,0,1:T(8,128)}, u32[]{:S(2)}, u32[]{:S(2)}) %collective-permute-start.2) | collective-permute-done | bytes 2097184 | tf_op jit(solution)/shard_map/ppermute | solution.py:81
  279.1 4.0 add.126
  286.2 4.8 fusion.62
  292.2 38.1 %collective-permute-done.3 = f32[32,128,128]{2,0,1:T(8,128)} collective-permute-done((f32[32,128,128]{2,0,1:T(8,128)}, f32[32,128,128]{2,0,1:T(8,128)}, u32[]{:S(2)}, u32[]{:S(2)}) %collective-permute-start.3) | collective-permute-done | bytes 2097184 | tf_op jit(solution)/shard_map/ppermute | solution.py:81
  330.3 3.4 fusion.37
  333.7 5.4 bitcast_subtract_fusion.3
  339.1 4.4 fusion.42
  346.9 45.1 %collective-permute-done.4 = f32[32,128,128]{2,0,1:T(8,128)S(1)} collective-permute-done((f32[32,128,128]{2,0,1:T(8,128)S(1)}, f32[32,128,128]{2,0,1:T(8,128)S(1)}, u32[]{:S(2)}, u32[]{:S(2)}) %collective-permute-start.4) | collective-permute-done | bytes 2097184 | tf_op jit(solution)/shard_map/ppermute | solution.py:81
  392.6 43.1 %collective-permute-done.5 = f32[32,128,128]{2,0,1:T(8,128)S(1)} collective-permute-done((f32[32,128,128]{2,0,1:T(8,128)S(1)}, f32[32,128,128]{2,0,1:T(8,128)S(1)}, u32[]{:S(2)}, u32[]{:S(2)}) %collective-permute-start.5) | collective-permute-done | bytes 2097184 | tf_op jit(solution)/shard_map/ppermute | solution.py:81
  437.1 45.1 %collective-permute-done.6 = f32[32,128,128]{2,0,1:T(8,128)S(1)} collective-permute-done((f32[32,128,128]{2,0,1:T(8,128)S(1)}, f32[32,128,128]{2,0,1:T(8,128)S(1)}, u32[]{:S(2)}, u32[]{:S(2)}) %collective-permute-start.6) | collective-permute-done | bytes 2097184 | tf_op jit(solution)/shard_map/ppermute | solution.py:81
  486.6 35.1 %collective-permute-done.7 = f32[32,128,128]{2,0,1:T(8,128)S(1)} collective-permute-done((f32[32,128,128]{2,0,1:T(8,128)S(1)}, f32[32,128,128]{2,0,1:T(8,128)S(1)}, u32[]{:S(2)}, u32[]{:S(2)}) %collective-permute-start.7) | collective-permute-done | bytes 2097184 | tf_op jit(solution)/shard_map/ppermute | solution.py:81
  523.0 4.5 bitcast_subtract_fusion.2
  527.5 4.0 fusion.45
  531.5 2.7 fusion.26
  536.5 37.4 %collective-permute-done.8 = f32[32,128,128]{2,0,1:T(8,128)S(1)} collective-permute-done((f32[32,128,128]{2,0,1:T(8,128)S(1)}, f32[32,128,128]{2,0,1:T(8,128)S(1)}, u32[]{:S(2)}, u32[]{:S(2)}) %collective-permute-start.8) | collective-permute-done | bytes 2097184 | tf_op jit(solution)/shard_map/ppermute | solution.py:81
  574.4 12.2 %collective-permute-start.9 = (f32[32,128,128]{2,0,1:T(8,128)S(1)}, f32[32,128,128]{2,0,1:T(8,128)S(1)}, u32[]{:S(2)}, u32[]{:S(2)}) collective-permute-start(f32[32,128,128]{2,0,1:T(8,128)S(1)} %add.138), channel_id=1, source_target_pairs={{0,32},{16,48},{32,0},{48,16},{64,96},{80,112},{96,64},{112,80},{1... | collective-permute-start | bytes 6291464 | tf_op jit(solution)/shard_map/ppermute | solution.py:81
  586.7 38.9 %collective-permute-done.9 = f32[32,128,128]{2,0,1:T(8,128)S(1)} collective-permute-done((f32[32,128,128]{2,0,1:T(8,128)S(1)}, f32[32,128,128]{2,0,1:T(8,128)S(1)}, u32[]{:S(2)}, u32[]{:S(2)}) %collective-permute-start.9) | collective-permute-done | bytes 2097184 | tf_op jit(solution)/shard_map/ppermute | solution.py:81
  628.5 39.9 %collective-permute-done.10 = f32[32,128,128]{2,0,1:T(8,128)S(1)} collective-permute-done((f32[32,128,128]{2,0,1:T(8,128)S(1)}, f32[32,128,128]{2,0,1:T(8,128)S(1)}, u32[]{:S(2)}, u32[]{:S(2)}) %collective-permute-start.10) | collective-permute-done | bytes 2097184 | tf_op jit(solution)/shard_map/ppermute | solution.py:81
  668.9 8.7 %collective-permute-start.11 = (f32[32,128,128]{2,0,1:T(8,128)S(1)}, f32[32,128,128]{2,0,1:T(8,128)S(1)}, u32[]{:S(2)}, u32[]{:S(2)}) collective-permute-start(f32[32,128,128]{2,0,1:T(8,128)S(1)} %add.140), channel_id=1, source_target_pairs={{0,128},{16,144},{32,160},{48,176},{64,192},{80,208},{96,224},{112... | collective-permute-start | bytes 6291464 | tf_op jit(solution)/shard_map/ppermute | solution.py:81
  681.3 38.1 %collective-permute-done.11 = f32[32,128,128]{2,0,1:T(8,128)S(1)} collective-permute-done((f32[32,128,128]{2,0,1:T(8,128)S(1)}, f32[32,128,128]{2,0,1:T(8,128)S(1)}, u32[]{:S(2)}, u32[]{:S(2)}) %collective-permute-start.11) | collective-permute-done | bytes 2097184 | tf_op jit(solution)/shard_map/ppermute | solution.py:81
  720.6 6.0 fusion.22
  (61 shorter events, 44.7 us)
Async XLA Ops:
  0.0 233.4 %copy-start = (bf16[32,128,128]{2,1,0:T(8,128)(2,1)S(1)}, bf16[32,128,128]{2,1,0:T(8,128)(2,1)}, u32[]{:S(2)}) copy-start(bf16[32,128,128]{2,1,0:T(8,128)(2,1)} %param.13) | copy-start | bytes 3145732
  20.6 101.1 %all-to-all-start = ((bf16[16,2,512,128]{2,3,1,0:T(8,128)(2,1)}), bf16[16,2,512,128]{2,3,1,0:T(8,128)(2,1)}, u32[]{:S(2)}, u32[]{:S(2)}) async-start(bf16[16,2,512,128]{2,3,1,0:T(8,128)(2,1)} %copy.18), calls=%async_computation | async-start | bytes 8388608 | tf_op jit(solution)/shard_map/all_to_all | solution.py:48
  29.2 92.5 %copy-start.2 = (f32[1,1,32,128,128]{4,3,2,1,0:T(8,128)S(1)}, f32[1,1,32,128,128]{4,3,2,1,0:T(8,128)}, u32[]{:S(2)}) copy-start(f32[1,1,32,128,128]{4,3,2,1,0:T(8,128)} %param.15) | copy-start | bytes 6291460
  121.7 4.9 copy-start.3
  126.7 4.5 copy-start.5
  133.7 47.9 %collective-permute-start = (f32[32,128,128]{2,0,1:T(8,128)S(1)}, f32[32,128,128]{2,0,1:T(8,128)S(1)}, u32[]{:S(2)}, u32[]{:S(2)}) collective-permute-start(f32[32,128,128]{2,0,1:T(8,128)S(1)} %fusion.30), channel_id=1, source_target_pairs={{0,16},{16,0},{32,48},{48,32},{64,80},{80,64},{96,112},{112,96},{1... | collective-permute-start | bytes 6291464 | tf_op jit(solution)/shard_map/ppermute | solution.py:81
  182.1 48.8 %collective-permute-start.1 = (f32[32,128,128]{2,0,1:T(8,128)S(1)}, f32[32,128,128]{2,0,1:T(8,128)S(1)}, u32[]{:S(2)}, u32[]{:S(2)}) collective-permute-start(f32[32,128,128]{2,0,1:T(8,128)S(1)} %add.124), channel_id=1, source_target_pairs={{0,32},{16,48},{32,0},{48,16},{64,96},{80,112},{96,64},{112,80},{1... | collective-permute-start | bytes 6291464 | tf_op jit(solution)/shard_map/ppermute | solution.py:81
  232.7 46.4 %collective-permute-start.2 = (f32[32,128,128]{2,0,1:T(8,128)}, f32[32,128,128]{2,0,1:T(8,128)}, u32[]{:S(2)}, u32[]{:S(2)}) collective-permute-start(f32[32,128,128]{2,0,1:T(8,128)} %add.125), channel_id=1, source_target_pairs={{0,64},{16,80},{32,96},{48,112},{64,0},{80,16},{96,32},{112,48},{1... | collective-permute-start | bytes 6291464 | tf_op jit(solution)/shard_map/ppermute | solution.py:81
  237.4 48.8 %all-to-all-start.1 = ((bf16[16,2,128,128]{3,2,1,0:T(8,128)(2,1)}), bf16[16,2,128,128]{3,2,1,0:T(8,128)(2,1)}, u32[]{:S(2)}, u32[]{:S(2)}) async-start(bf16[16,2,128,128]{3,2,1,0:T(8,128)(2,1)} %bitcast.130), calls=%async_computation.1 | async-start | bytes 2097152 | tf_op jit(solution)/shard_map/all_to_all | solution.py:49
  283.1 47.2 %collective-permute-start.3 = (f32[32,128,128]{2,0,1:T(8,128)}, f32[32,128,128]{2,0,1:T(8,128)}, u32[]{:S(2)}, u32[]{:S(2)}) collective-permute-start(f32[32,128,128]{2,0,1:T(8,128)} %add.126), channel_id=1, source_target_pairs={{0,128},{16,144},{32,160},{48,176},{64,192},{80,208},{96,224},{112... | collective-permute-start | bytes 6291464 | tf_op jit(solution)/shard_map/ppermute | solution.py:81
  286.2 4.8 copy-start.7
  292.2 41.5 %copy-start.4 = (f32[1,1,32,128,128]{4,3,2,1,0:T(8,128)S(1)}, f32[1,1,32,128,128]{4,3,2,1,0:T(8,128)}, u32[]{:S(2)}) copy-start(f32[1,1,32,128,128]{4,3,2,1,0:T(8,128)} %param.14) | copy-start | bytes 6291460
  292.2 41.5 %copy-start.6 = (f32[32,128,128]{2,1,0:T(8,128)S(1)}, f32[32,128,128]{2,1,0:T(8,128)}, u32[]{:S(2)}) copy-start(f32[32,128,128]{2,1,0:T(8,128)} %copy-done.5) | copy-start | bytes 6291460
  346.0 46.0 %collective-permute-start.4 = (f32[32,128,128]{2,0,1:T(8,128)S(1)}, f32[32,128,128]{2,0,1:T(8,128)S(1)}, u32[]{:S(2)}, u32[]{:S(2)}) collective-permute-start(f32[32,128,128]{2,0,1:T(8,128)S(1)} %fusion.28), channel_id=1, source_target_pairs={{0,16},{16,0},{32,48},{48,32},{64,80},{80,64},{96,112},{112,96},{1... | collective-permute-start | bytes 6291464 | tf_op jit(solution)/shard_map/ppermute | solution.py:81
  392.5 43.2 %collective-permute-start.5 = (f32[32,128,128]{2,0,1:T(8,128)S(1)}, f32[32,128,128]{2,0,1:T(8,128)S(1)}, u32[]{:S(2)}, u32[]{:S(2)}) collective-permute-start(f32[32,128,128]{2,0,1:T(8,128)S(1)} %add.131), channel_id=1, source_target_pairs={{0,32},{16,48},{32,0},{48,16},{64,96},{80,112},{96,64},{112,80},{1... | collective-permute-start | bytes 6291464 | tf_op jit(solution)/shard_map/ppermute | solution.py:81
  436.3 45.9 %collective-permute-start.6 = (f32[32,128,128]{2,0,1:T(8,128)S(1)}, f32[32,128,128]{2,0,1:T(8,128)S(1)}, u32[]{:S(2)}, u32[]{:S(2)}) collective-permute-start(f32[32,128,128]{2,0,1:T(8,128)S(1)} %add.132), channel_id=1, source_target_pairs={{0,64},{16,80},{32,96},{48,112},{64,0},{80,16},{96,32},{112,48},{1... | collective-permute-start | bytes 6291464 | tf_op jit(solution)/shard_map/ppermute | solution.py:81
  482.6 39.1 %collective-permute-start.7 = (f32[32,128,128]{2,0,1:T(8,128)S(1)}, f32[32,128,128]{2,0,1:T(8,128)S(1)}, u32[]{:S(2)}, u32[]{:S(2)}) collective-permute-start(f32[32,128,128]{2,0,1:T(8,128)S(1)} %add.133), channel_id=1, source_target_pairs={{0,128},{16,144},{32,160},{48,176},{64,192},{80,208},{96,224},{112... | collective-permute-start | bytes 6291464 | tf_op jit(solution)/shard_map/ppermute | solution.py:81
  534.1 39.8 %collective-permute-start.8 = (f32[32,128,128]{2,0,1:T(8,128)S(1)}, f32[32,128,128]{2,0,1:T(8,128)S(1)}, u32[]{:S(2)}, u32[]{:S(2)}) collective-permute-start(f32[32,128,128]{2,0,1:T(8,128)S(1)} %fusion.26), channel_id=1, source_target_pairs={{0,16},{16,0},{32,48},{48,32},{64,80},{80,64},{96,112},{112,96},{1... | collective-permute-start | bytes 6291464 | tf_op jit(solution)/shard_map/ppermute | solution.py:81
  574.4 51.1 %collective-permute-start.9 = (f32[32,128,128]{2,0,1:T(8,128)S(1)}, f32[32,128,128]{2,0,1:T(8,128)S(1)}, u32[]{:S(2)}, u32[]{:S(2)}) collective-permute-start(f32[32,128,128]{2,0,1:T(8,128)S(1)} %add.138), channel_id=1, source_target_pairs={{0,32},{16,48},{32,0},{48,16},{64,96},{80,112},{96,64},{112,80},{1... | collective-permute-start | bytes 6291464 | tf_op jit(solution)/shard_map/ppermute | solution.py:81
  626.0 42.4 %collective-permute-start.10 = (f32[32,128,128]{2,0,1:T(8,128)S(1)}, f32[32,128,128]{2,0,1:T(8,128)S(1)}, u32[]{:S(2)}, u32[]{:S(2)}) collective-permute-start(f32[32,128,128]{2,0,1:T(8,128)S(1)} %add.139), channel_id=1, source_target_pairs={{0,64},{16,80},{32,96},{48,112},{64,0},{80,16},{96,32},{112,48},{1... | collective-permute-start | bytes 6291464 | tf_op jit(solution)/shard_map/ppermute | solution.py:81
  668.9 50.5 %collective-permute-start.11 = (f32[32,128,128]{2,0,1:T(8,128)S(1)}, f32[32,128,128]{2,0,1:T(8,128)S(1)}, u32[]{:S(2)}, u32[]{:S(2)}) collective-permute-start(f32[32,128,128]{2,0,1:T(8,128)S(1)} %add.140), channel_id=1, source_target_pairs={{0,128},{16,144},{32,160},{48,176},{64,192},{80,208},{96,224},{112... | collective-permute-start | bytes 6291464 | tf_op jit(solution)/shard_map/ppermute | solution.py:81
  720.6 6.0 copy-start.1
